TPU v7x, 256 devices: a whole 4x4x8 slice. The times are simulated.
256 devices in a mesh: seq: 16 (over y_lo, z), dp: 16 (over x, y_hi, core).
Axes of the slice: x: 4, y: 4 (y_hi: 2, y_lo: 2; y = y_hi * 2 + y_lo), z: 8, core: 2. Of those that a mesh axis runs over, the one named last changes fastest.
Arguments:
- layer_rows: bfloat16 [16, 2048, 1024], P('dp', 'seq'), may hold values from -6 to 6
- doc_ids: int32 [16, 2048], P('dp', 'seq'), may hold values from 0 to 5, never falling along the last dimension, each value on 1 to 1024 neighbouring positions
- packing: int32 [16, 16], P('dp'), may hold values from 0 to 15, each once within a row
- norm_gain: float32 [1024], replicated, may hold values from 0.1 to 1.9
- w_qkv: bfloat16 [1024, 3072], replicated, may hold values from -0.1875 to 0.1875
- d_attn: bfloat16 [16, 2048, 1024], P('dp', 'seq'), may hold values from -6 to 6
Outputs:
- d_input: bfloat16 [16, 2048, 1024], P('dp', 'seq')
- w_grad: float32 [1024, 3072], P('seq')
Inputs may be any that keep to these rules, and one draw needn't show every extreme that they name: `doc_ids`: in each group the song numbers never fall along the initial order; every number occurs, and one song spans exactly 1024 frames. `packing`: each group's row names every block number once.
All inputs are finite; a program needn't handle non-finite values.
Results may differ from a plain program's by a relative error of at most 0.024.
Values may be sent and summed in bfloat16 or wider, within the bound.
No kernel may reach another device: no remote copies, remote signals or barrier semaphores. Data moves between devices by JAX's collectives and lax.ppermute only.
A program may use at most 128 MiB of HBM per device.

v0:
```python
import math
import jax
import jax.numpy as jnp
from jax import lax
from jax.sharding import PartitionSpec as P

HEADS = 8
HEAD = 128
BLOCK = 128


def rounded(value):
    return lax.optimization_barrier(value.astype(jnp.bfloat16)).astype(jnp.float32)


def normalize(frames, norm_gain):
    values = frames.astype(jnp.float32)
    inverse = lax.rsqrt(jnp.mean(values * values, axis=-1, keepdims=True) + 1e-05)
    unit_rows = values * inverse
    return (inverse, unit_rows, (unit_rows * norm_gain).astype(jnp.bfloat16))


def body(layer_rows, doc_ids, packing, norm_gain, w_qkv, d_attn):
    shards = lax.axis_size("seq")
    my_index = lax.axis_index("seq")
    frames = layer_rows[0]
    tok_rows = frames.shape[0]
    head_cols = HEADS * HEAD
    total_keys = tok_rows * shards
    block_order = packing[0]
    key_pos = (block_order[:, None] * BLOCK + jnp.arange(BLOCK, dtype=jnp.int32)[None, :]).reshape(
        total_keys
    )
    first_own = my_index * tok_rows
    my_pos = lax.dynamic_slice_in_dim(key_pos, first_own, tok_rows, 0)
    doc_low = doc_ids[0].astype(jnp.bfloat16)
    pieces = (
        lax.all_gather(frames, "seq", axis=0, tiled=True),
        lax.all_gather(doc_low, "seq", axis=0, tiled=True),
    )
    length = pieces[0].shape[0]
    inside = (my_pos >= 0) & (my_pos < length)
    clipped = jnp.clip(my_pos, 0, length - 1)
    new_rows = jnp.where(
        inside[:, None], jnp.take(pieces[0], clipped, axis=0), jnp.zeros_like(frames)
    )
    new_docs = jnp.where(inside, jnp.take(pieces[1], clipped, axis=0), jnp.zeros_like(doc_low))
    inverse, unit_rows, normed = normalize(new_rows, norm_gain)
    projected = jnp.dot(normed, w_qkv, preferred_element_type=jnp.float32).astype(jnp.bfloat16)
    queries = projected[:, :head_cols]
    all_keys, all_values, key_docs_low = (
        lax.all_gather(projected[:, head_cols : 2 * head_cols], "seq", axis=0, tiled=True),
        lax.all_gather(projected[:, 2 * head_cols :], "seq", axis=0, tiled=True),
        lax.all_gather(new_docs, "seq", axis=0, tiled=True),
    )
    key_docs = key_docs_low.astype(jnp.int32)
    my_docs = lax.dynamic_slice_in_dim(key_docs, first_own, tok_rows, 0)
    factor = 1.0 / math.sqrt(HEAD)
    q_heads = queries.reshape(tok_rows, HEADS, HEAD)
    grad_heads = d_attn[0].reshape(tok_rows, HEADS, HEAD)
    group_count = total_keys // total_keys

    def key_slab(group_idx):
        first_key = group_idx * total_keys
        slab_keys = all_keys.reshape(total_keys, HEADS, HEAD)
        slab_values = all_values.reshape(total_keys, HEADS, HEAD)
        allowed = (my_docs[:, None] == key_docs[None, :]) & (key_pos[None, :] <= my_pos[:, None])
        return (first_key, slab_keys, slab_values, allowed)

    def exp_scores(query_part, slab_keys, allowed):
        scores = (
            jnp.einsum("qhd,khd->hqk", query_part, slab_keys, preferred_element_type=jnp.float32)
            * factor
        )
        return jnp.where(allowed[None], jnp.exp(scores), jnp.float32(0.0))

    def add_denominator(group_idx, running):
        first_key, slab_keys, slab_values, allowed = key_slab(group_idx)
        return running + jnp.sum(exp_scores(q_heads, slab_keys, allowed), axis=-1)

    denominator = lax.fori_loop(
        0, group_count, add_denominator, jnp.zeros((HEADS, tok_rows), jnp.float32)
    )

    def probabilities(slab_keys, allowed):
        attn_prob = exp_scores(q_heads, slab_keys, allowed) / denominator[:, :, None]
        return (attn_prob, attn_prob.astype(jnp.bfloat16))

    def add_output(group_idx, running):
        first_key, slab_keys, slab_values, allowed = key_slab(group_idx)

        def compute():
            attn_prob, prob_low = probabilities(slab_keys, allowed)
            return jnp.einsum(
                "hqk,khd->qhd", prob_low, slab_values, preferred_element_type=jnp.float32
            )

        return running + compute()

    outputs = lax.fori_loop(
        0, group_count, add_output, jnp.zeros((tok_rows, HEADS, HEAD), jnp.float32)
    )
    row_delta = jnp.sum(grad_heads.astype(jnp.float32) * outputs, axis=-1).T

    def slab_backward(slab_keys, slab_values, allowed):
        attn_prob, prob_low = probabilities(slab_keys, allowed)
        grad_prob = jnp.einsum(
            "qhd,khd->hqk", grad_heads, slab_values, preferred_element_type=jnp.float32
        )
        dscore = (attn_prob * (grad_prob - row_delta[:, :, None])).astype(jnp.bfloat16)
        dq_part = (
            jnp.einsum("hqk,khd->qhd", dscore, slab_keys, preferred_element_type=jnp.float32)
            * factor
        )
        return (dq_part, dscore, prob_low)

    def add_grads(group_idx, running):
        dq_sum, kv_grads = running
        first_key, slab_keys, slab_values, allowed = key_slab(group_idx)

        def compute():
            dq_part, dscore, prob_low = slab_backward(slab_keys, slab_values, allowed)
            dk_part = (
                jnp.einsum("hqk,qhd->khd", dscore, q_heads, preferred_element_type=jnp.float32)
                * factor
            )
            dv_part = jnp.einsum(
                "hqk,qhd->khd", prob_low, grad_heads, preferred_element_type=jnp.float32
            )
            return (
                dq_part,
                jnp.concatenate(
                    [
                        dk_part.reshape(total_keys, head_cols),
                        dv_part.reshape(total_keys, head_cols),
                    ],
                    axis=1,
                ),
            )

        dq_part, kv_part = compute()
        return (dq_sum + dq_part, kv_part)

    dq_sum, kv_grads = lax.fori_loop(
        0,
        group_count,
        add_grads,
        (
            jnp.zeros((tok_rows, HEADS, HEAD), jnp.float32),
            jnp.zeros((total_keys, 2 * head_cols), jnp.float32),
        ),
    )
    summed = lax.psum_scatter(
        rounded(kv_grads).astype(jnp.bfloat16), "seq", scatter_dimension=0, tiled=True
    ).astype(jnp.float32)
    grad_qkv = jnp.concatenate([dq_sum.reshape(tok_rows, head_cols), summed], axis=1).astype(
        jnp.bfloat16
    )
    d_normed = lax.dot_general(
        grad_qkv, w_qkv, (((1,), (1,)), ((), ())), preferred_element_type=jnp.float32
    )
    gained = d_normed * norm_gain
    d_frames = (
        inverse * (gained - unit_rows * jnp.mean(gained * unit_rows, axis=-1, keepdims=True))
    ).astype(jnp.bfloat16)
    w_part = lax.psum_scatter(
        rounded(
            lax.dot_general(
                normed, grad_qkv, (((0,), (0,)), ((), ())), preferred_element_type=jnp.float32
            )
        ).astype(jnp.bfloat16),
        "seq",
        scatter_dimension=0,
        tiled=True,
    )
    w_total = lax.psum(w_part, "dp").astype(jnp.float32)
    w_grad = w_total * (1.0 / math.sqrt(total_keys * lax.axis_size("dp")))
    return (d_frames[None], w_grad)


def solution(mesh):
    return jax.shard_map(
        body,
        mesh=mesh,
        in_specs=(
            P("dp", "seq", None),
            P("dp", "seq"),
            P("dp", None),
            P(),
            P(),
            P("dp", "seq", None),
        ),
        out_specs=(P("dp", "seq", None), P("seq", None)),
        check_vma=False,
    )
```

profile of v0, /device:TPU:1, one launch (start us, length us, event | category | flops | bytes accessed | tf_op | source)
XLA Modules:
  0.0 635.3 jit_solution(11670641613337491043)
XLA Ops:
  8.8 71.3 %all-gather.11.cloned.1.call-done = bf16[1,2048,1024]{2,1,0:T(8,128)(2,1)} async-done(((bf16[1,128,1024]{2,1,0:T(8,128)(2,1)}), bf16[1,2048,1024]{2,1,0:T(8,128)(2,1)}) %all-gather.11.cloned.1.call-update) | async-done | bytes 4194320 | tf_op jit(solution)/shard_map/all_gather | solution.py:38
  80.1 3.8 gather_fusion
  84.1 3.9 convolution_convert_fusion.2
  89.7 25.4 %all-gather.1 = bf16[1,2048]{1,0:T(2,128)(2,1)S(1)} all-gather(bf16[1,128]{1,0:T(2,128)(2,1)S(1)} %convert_element_type.50), channel_id=3, replica_groups=mesh['seq'=16,'dp'=16] {'seq'}, dimensions={1}, use_global_device_ids=true | all-gather | bytes 4352 | tf_op jit(solution)/shard_map/all_gather | solution.py:39
  116.5 24.9 %all-gather.2 = bf16[16,1,128]{2,1,0:T(2,128)(2,1)S(1)} all-gather(bf16[1,1,128]{2,1,0:T(2,128)(2,1)S(1)} %select_bitcast_fusion), channel_id=1, replica_groups=mesh['seq'=16,'dp'=16] {'seq'}, dimensions={0}, use_global_device_ids=true | all-gather | bytes 4352 | tf_op jit(solution)/shard_map/all_gather | solution.py:54
  142.2 21.2 %all-gather.7.cloned.1.call-done = bf16[2048,1024]{1,0:T(8,128)(2,1)} async-done(((bf16[128,1024]{1,0:T(8,128)(2,1)}), bf16[2048,1024]{1,0:T(8,128)(2,1)}) %all-gather.7.cloned.1.call-update) | async-done | bytes 4194320 | tf_op jit(solution)/shard_map/all_gather | solution.py:52
  163.4 6.5 %copy.39 = bf16[2048,1024]{0,1:T(8,128)(2,1)} copy(bf16[2048,1024]{1,0:T(8,128)(2,1)} %all-gather.7.cloned.1.call-done) | data formatting | bytes 8388608 | tf_op jit(solution)/shard_map/while/body/eval_jaxpr/reshape | solution.py:65
  169.9 5.1 fusion.2
  175.0 3.2 copy-done
  178.2 4.5 convolution_convert_fusion.1
  182.8 55.8 %all-gather.9.cloned.1.call-done = bf16[2048,1024]{1,0:T(8,128)(2,1)} async-done(((bf16[128,1024]{1,0:T(8,128)(2,1)}), bf16[2048,1024]{1,0:T(8,128)(2,1)}) %all-gather.9.cloned.1.call-update) | async-done | bytes 4194320 | tf_op jit(solution)/shard_map/all_gather | solution.py:53
  238.5 6.5 %copy.41 = bf16[2048,1024]{0,1:T(8,128)(2,1)} copy(bf16[2048,1024]{1,0:T(8,128)(2,1)} %all-gather.9.cloned.1.call-done) | data formatting | bytes 8388608 | tf_op jit(solution)/shard_map/while/body/eval_jaxpr/reshape | solution.py:66
  245.0 7.3 %fusion.13 = f32[128,8]{0,1:T(8,128)S(1)} fusion(bf16[2048,8,128]{0,2,1:T(8,128)(2,1)} %bitcast.50, bf16[128,8,128]{0,2,1:T(8,128)(2,1)S(1)} %bitcast.59, f32[8,128,2048]{2,1,0:T(8,128)} %copy-done, f32[8,128]{1,0:T(8,128)S(1)} %get-tuple-element.73, pred[128,2048]{1,0:T(8,128)(4,1)S(1)} %compare_and_fusion), kind=kOutput, calls=%fused_computation.20 | convolution fusion | flops 545651712 | bytes 13115392 | tf_op jit(solution)/shard_map/while/body/eval_jaxpr/hqk,khd->qhd/dot_general | solution.py:94
  252.3 5.2 fusion
  257.6 2.0 copy-done.2
  259.5 3.2 multiply_convert_fusion
  262.7 8.3 %pad_maximum_fusion = bf16[2048,2048]{0,1:T(8,128)(2,1)} fusion(bf16[2048,1024]{0,1:T(8,128)(2,1)} %bitcast.52, bf16[2048,1024]{0,1:T(8,128)(2,1)} %bitcast.49), kind=kLoop, calls=%fused_computation.2 | loop fusion | flops 16777216 | bytes 16777216 | tf_op jit(solution)/shard_map/while/body/eval_jaxpr/concatenate | solution.py:132
  271.1 12.2 %copy.37 = bf16[2048,2048]{1,0:T(8,128)(2,1)} copy(bf16[2048,2048]{0,1:T(8,128)(2,1)} %pad_maximum_fusion) | data formatting | bytes 16777216
  283.6 4.7 fusion.12
  288.3 103.2 %reduce-scatter.7.cloned.1.call-done = bf16[128,2048]{1,0:T(8,128)(2,1)} async-done(((bf16[2048,2048]{1,0:T(8,128)(2,1)}), bf16[128,2048]{1,0:T(8,128)(2,1)}) %reduce-scatter.7.cloned.1.call-update) | async-done | bytes 524304
  392.9 4.6 convolution_convert_fusion
  397.6 5.1 fusion.20
  402.7 71.0 %reduce-scatter.5.cloned.1.call-done = bf16[64,3072]{1,0:T(8,128)(2,1)} async-done(((bf16[1024,3072]{1,0:T(8,128)(2,1)}), bf16[64,3072]{1,0:T(8,128)(2,1)}) %reduce-scatter.5.cloned.1.call-update) | async-done | bytes 393232 | tf_op jit(solution)/shard_map/reduce_scatter | solution.py:166
  474.7 151.8 %all-reduce.2.cloned.1.call-done = bf16[64,3072]{1,0:T(8,128)(2,1)} async-done(((bf16[64,3072]{1,0:T(8,128)(2,1)}), bf16[64,3072]{1,0:T(8,128)(2,1)}) %all-reduce.2.cloned.1.call-update) | async-done | bytes 393232 | tf_op jit(solution)/shard_map/psum | solution.py:176
  (44 shorter events, 10.1 us)
Async XLA Ops:
  7.2 72.9 %all-gather.11.cloned.1.call-start = ((), (), s32[]{:S(2)}) async-start(), calls=%async_computation.6 | async-start | bytes 4456448 | tf_op jit(solution)/shard_map/all_gather | solution.py:38
  7.9 155.5 %all-gather.7.cloned.1.call-start = ((), (), s32[]{:S(2)}) async-start(), calls=%async_computation.2 | async-start | bytes 4456448 | tf_op jit(solution)/shard_map/all_gather | solution.py:52
  84.1 5.6 copy-start.5
  84.1 57.4 %copy-start.3 = (bf16[1,128,1024]{2,1,0:T(8,128)(2,1)S(1)}, bf16[1,128,1024]{2,1,0:T(8,128)(2,1)}, u32[]{:S(2)}) copy-start(bf16[1,128,1024]{2,1,0:T(8,128)(2,1)} %param.11) | copy-start | bytes 786436
  88.9 149.6 %all-gather.9.cloned.1.call-start = ((), (), s32[]{:S(2)}) async-start(), calls=%async_computation.3 | async-start | bytes 4456448 | tf_op jit(solution)/shard_map/all_gather | solution.py:53
  89.7 301.9 %reduce-scatter.7.cloned.1.call-start = ((), (), s32[]{:S(2)}) async-start(), calls=%async_computation.7 | async-start | bytes 8912896
  175.0 3.2 copy-start
  245.0 7.3 %copy-start.1 = (f32[8,128,2048]{2,1,0:T(8,128)S(1)}, f32[8,128,2048]{2,1,0:T(8,128)}, u32[]{:S(2)}) copy-start(f32[8,128,2048]{2,1,0:T(8,128)} %copy-done) | copy-start | bytes 25165828
  257.6 2.0 copy-start.2
  283.3 109.6 %copy-start.4 = (f32[1024]{0:T(1024)S(1)}, f32[1024]{0:T(1024)}, u32[]{:S(2)}) copy-start(f32[1024]{0:T(1024)} %param.9) | copy-start | bytes 12292
  283.3 190.4 %reduce-scatter.5.cloned.1.call-start = ((), (), s32[]{:S(2)}) async-start(), calls=%async_computation.4 | async-start | bytes 6684672 | tf_op jit(solution)/shard_map/reduce_scatter | solution.py:166
  397.6 228.9 %all-reduce.2.cloned.1.call-start = ((), (), s32[]{:S(2)}) async-start(), calls=%async_computation.5 | async-start | bytes 786432 | tf_op jit(solution)/shard_map/psum | solution.py:176
Sparse Core Ops, SparseCore 0:
  9.8 70.2 all-gather.10
  89.0 74.2 all-gather.6
  165.7 72.7 all-gather.8
  283.5 108.0 reduce-scatter.6
  397.7 76.0 reduce-scatter.4
  476.2 150.2 all-reduce.1
where the time goes:
time: 636 us; the launch traced here: 635 us
  waiting for transfers between devices  476 us (75%)
  blocking collectives  50.4 us (8%)
  matrix products  43.7 us (7%)
  local copies, waits for them, and re-layouts  38.1 us (6%)
  between operations  14.3 us (2%)
  other arithmetic  12.6 us (2%)
    psum x1, waiting for transfers between devices, body(): w_total = lax.psum(w_part, 'dp').astype(jnp.float32)  152 us
    unnamed x7, waiting for transfers between devices  105 us
    all_gather x1, waiting for transfers between devices, body(): lax.all_gather(frames, 'seq', axis=0, tiled=True)  71.3 us
    reduce_scatter x1, waiting for transfers between devices, body(): lax.psum_scatter(rounded(lax.dot_general(normed, grad_qkv, (((0,), (0,)),...  71 us
    all_gather x1, waiting for transfers between devices, body(): lax.all_gather(projected[:, 2 * head_cols:], 'seq', axis=0, tiled=True)  55.8 us
    all_gather x1, blocking collectives, body(): lax.all_gather(doc_low, 'seq', axis=0, tiled=True)  25.4 us
    all_gather x1, blocking collectives, body(): lax.all_gather(new_docs, 'seq', axis=0, tiled=True)  24.9 us
    all_gather x1, waiting for transfers between devices, body(): lax.all_gather(projected[:, head_cols:2 * head_cols], 'seq', axis=0, tile...  21.2 us
  transfers between devices with their start and end apart: 6, of which 6 were waited for; matrix products, arithmetic and copies ran while one was open for 5% of the time, Pallas kernels for 0%

commit v1 on v0

--- a/solution.py
+++ b/solution.py
@@ -36,7 +36,9 @@
     doc_low = doc_ids[0].astype(jnp.bfloat16)
     pieces = (
         lax.all_gather(frames, "seq", axis=0, tiled=True),
-        lax.all_gather(doc_low, "seq", axis=0, tiled=True),
+        jnp.concatenate(
+            lax.all_to_all(jnp.stack([doc_low] * lax.axis_size("seq")), "seq", 0, 0), axis=0
+        ),
     )
     length = pieces[0].shape[0]
     inside = (my_pos >= 0) & (my_pos < length)

time: 636 us -> 636 us (level)
  blocking collectives: 50.4 us -> 24.7 us
  waiting for transfers between devices: 476 us -> 497 us
    all_gather x1 -> x0, blocking collectives: 25.4 us -> none  [body(): lax.all_gather(doc_low, 'seq', axis=0, tiled=True)]
    all_gather x1, waiting for transfers between devices: 21.2 us -> 35 us  [body(): lax.all_gather(projected[:, head_cols:2 * head_cols], 'seq', axis=0, tile...]
    all_to_all x0 -> x1, waiting for transfers between devices: none -> 7.05 us  [body(): lax.all_to_all(jnp.stack([doc_low] * lax.axis_size('seq')), 'seq', 0, 0)]
  transfers between devices with their start and end apart: 6 -> 7, of which waited for: 6 -> 7; matrix products, arithmetic and copies ran while one was open for 5% -> 5% of each run, Pallas kernels for 0% -> 0%
where the time goes in v1:
time: 636 us; the launch traced here: 635 us
  waiting for transfers between devices  497 us (78%)
  matrix products  43.8 us (7%)
  local copies, waits for them, and re-layouts  38.7 us (6%)
  blocking collectives  24.7 us (4%)
  between operations  14.3 us (2%)
  other arithmetic  12.6 us (2%)
    psum x1, waiting for transfers between devices, body(): w_total = lax.psum(w_part, 'dp').astype(jnp.float32)  151 us
    unnamed x7, waiting for transfers between devices  105 us
    reduce_scatter x1, waiting for transfers between devices, body(): lax.psum_scatter(rounded(lax.dot_general(normed, grad_qkv, (((0,), (0,)),...  71.7 us
    all_gather x1, waiting for transfers between devices, body(): lax.all_gather(frames, 'seq', axis=0, tiled=True)  71.3 us
    all_gather x1, waiting for transfers between devices, body(): lax.all_gather(projected[:, 2 * head_cols:], 'seq', axis=0, tiled=True)  56.2 us
    all_gather x1, waiting for transfers between devices, body(): lax.all_gather(projected[:, head_cols:2 * head_cols], 'seq', axis=0, tile...  35 us
    all_gather x1, blocking collectives, body(): lax.all_gather(new_docs, 'seq', axis=0, tiled=True)  24.7 us
    unnamed x15, local copies, waits for them, and re-layouts  18.9 us
  transfers between devices with their start and end apart: 7, of which 7 were waited for; matrix products, arithmetic and copies ran while one was open for 5% of the time, Pallas kernels for 0%

profile of v1, /device:TPU:1, one launch (start us, length us, event | category | flops | bytes accessed | tf_op | source)
XLA Modules:
  0.0 635.2 jit_solution(13368393092581142258)
XLA Ops:
  8.8 71.3 %all-gather.10.cloned.1.call-done = bf16[1,2048,1024]{2,1,0:T(8,128)(2,1)} async-done(((bf16[1,128,1024]{2,1,0:T(8,128)(2,1)}), bf16[1,2048,1024]{2,1,0:T(8,128)(2,1)}) %all-gather.10.cloned.1.call-update) | async-done | bytes 4194320 | tf_op jit(solution)/shard_map/all_gather | solution.py:38
  80.1 3.8 gather_fusion
  84.1 3.9 convolution_convert_fusion.2
  90.3 3.5 all-to-all-start
  94.0 7.0 %all-to-all-done = bf16[16,1,128]{2,1,0:T(2,128)(2,1)S(1)} async-done(((bf16[16,1,128]{2,1,0:T(2,128)(2,1)}), bf16[16,1,128]{2,1,0:T(2,128)(2,1)S(1)}, u32[]{:S(2)}, u32[]{:S(2)}) %all-to-all-start) | async-done | bytes 4128 | tf_op jit(solution)/shard_map/all_to_all | solution.py:40
  102.4 24.7 %all-gather.1 = bf16[16,1,128]{2,1,0:T(2,128)(2,1)S(1)} all-gather(bf16[1,1,128]{2,1,0:T(2,128)(2,1)S(1)} %select_bitcast_fusion), channel_id=1, replica_groups=mesh['seq'=16,'dp'=16] {'seq'}, dimensions={0}, use_global_device_ids=true | all-gather | bytes 4352 | tf_op jit(solution)/shard_map/all_gather | solution.py:56
  127.6 35.0 %all-gather.6.cloned.1.call-done = bf16[2048,1024]{1,0:T(8,128)(2,1)} async-done(((bf16[128,1024]{1,0:T(8,128)(2,1)}), bf16[2048,1024]{1,0:T(8,128)(2,1)}) %all-gather.6.cloned.1.call-update) | async-done | bytes 4194320 | tf_op jit(solution)/shard_map/all_gather | solution.py:54
  162.6 6.5 %copy.39 = bf16[2048,1024]{0,1:T(8,128)(2,1)} copy(bf16[2048,1024]{1,0:T(8,128)(2,1)} %all-gather.6.cloned.1.call-done) | data formatting | bytes 8388608 | tf_op jit(solution)/shard_map/while/body/eval_jaxpr/reshape | solution.py:67
  169.1 5.1 fusion.2
  174.3 3.2 copy-done
  177.4 4.6 convolution_convert_fusion.1
  182.0 56.2 %all-gather.8.cloned.1.call-done = bf16[2048,1024]{1,0:T(8,128)(2,1)} async-done(((bf16[128,1024]{1,0:T(8,128)(2,1)}), bf16[2048,1024]{1,0:T(8,128)(2,1)}) %all-gather.8.cloned.1.call-update) | async-done | bytes 4194320 | tf_op jit(solution)/shard_map/all_gather | solution.py:55
  238.3 6.5 %copy.41 = bf16[2048,1024]{0,1:T(8,128)(2,1)} copy(bf16[2048,1024]{1,0:T(8,128)(2,1)} %all-gather.8.cloned.1.call-done) | data formatting | bytes 8388608 | tf_op jit(solution)/shard_map/while/body/eval_jaxpr/reshape | solution.py:68
  244.8 7.3 %fusion.13 = f32[128,8]{0,1:T(8,128)S(1)} fusion(bf16[2048,8,128]{0,2,1:T(8,128)(2,1)} %bitcast.54, bf16[128,8,128]{0,2,1:T(8,128)(2,1)S(1)} %bitcast.63, f32[8,128,2048]{2,1,0:T(8,128)} %copy-done, f32[8,128]{1,0:T(8,128)S(1)} %get-tuple-element.73, pred[128,2048]{1,0:T(8,128)(4,1)S(1)} %compare_and_fusion), kind=kOutput, calls=%fused_computation.20 | convolution fusion | flops 545651712 | bytes 13115392 | tf_op jit(solution)/shard_map/while/body/eval_jaxpr/hqk,khd->qhd/dot_general | solution.py:96
  252.1 5.2 fusion
  259.3 3.2 multiply_convert_fusion
  262.5 8.4 %pad_maximum_fusion = bf16[2048,2048]{0,1:T(8,128)(2,1)} fusion(bf16[2048,1024]{0,1:T(8,128)(2,1)} %bitcast.56, bf16[2048,1024]{0,1:T(8,128)(2,1)} %bitcast.53), kind=kLoop, calls=%fused_computation.2 | loop fusion | flops 16777216 | bytes 16777216 | tf_op jit(solution)/shard_map/while/body/eval_jaxpr/concatenate | solution.py:134
  270.8 12.2 %copy.37 = bf16[2048,2048]{1,0:T(8,128)(2,1)} copy(bf16[2048,2048]{0,1:T(8,128)(2,1)} %pad_maximum_fusion) | data formatting | bytes 16777216
  283.4 4.7 fusion.12
  288.1 103.5 %reduce-scatter.7.cloned.1.call-done = bf16[128,2048]{1,0:T(8,128)(2,1)} async-done(((bf16[2048,2048]{1,0:T(8,128)(2,1)}), bf16[128,2048]{1,0:T(8,128)(2,1)}) %reduce-scatter.7.cloned.1.call-update) | async-done | bytes 524304
  392.9 4.6 convolution_convert_fusion
  397.6 5.1 fusion.20
  402.7 71.7 %reduce-scatter.5.cloned.1.call-done = bf16[64,3072]{1,0:T(8,128)(2,1)} async-done(((bf16[1024,3072]{1,0:T(8,128)(2,1)}), bf16[64,3072]{1,0:T(8,128)(2,1)}) %reduce-scatter.5.cloned.1.call-update) | async-done | bytes 393232 | tf_op jit(solution)/shard_map/reduce_scatter | solution.py:168
  475.4 151.0 %all-reduce.2.cloned.1.call-done = bf16[64,3072]{1,0:T(8,128)(2,1)} async-done(((bf16[64,3072]{1,0:T(8,128)(2,1)}), bf16[64,3072]{1,0:T(8,128)(2,1)}) %all-reduce.2.cloned.1.call-update) | async-done | bytes 393232 | tf_op jit(solution)/shard_map/psum | solution.py:178
  (46 shorter events, 12.6 us)
Async XLA Ops:
  7.2 72.9 %all-gather.10.cloned.1.call-start = ((), (), s32[]{:S(2)}) async-start(), calls=%async_computation.7 | async-start | bytes 4456448 | tf_op jit(solution)/shard_map/all_gather | solution.py:38
  7.9 154.7 %all-gather.6.cloned.1.call-start = ((), (), s32[]{:S(2)}) async-start(), calls=%async_computation.3 | async-start | bytes 4456448 | tf_op jit(solution)/shard_map/all_gather | solution.py:54
  84.1 5.6 copy-start.5
  84.1 9.8 %copy-start.3 = (bf16[1,128,1024]{2,1,0:T(8,128)(2,1)S(1)}, bf16[1,128,1024]{2,1,0:T(8,128)(2,1)}, u32[]{:S(2)}) copy-start(bf16[1,128,1024]{2,1,0:T(8,128)(2,1)} %param.11) | copy-start | bytes 786436
  88.9 149.3 %all-gather.8.cloned.1.call-start = ((), (), s32[]{:S(2)}) async-start(), calls=%async_computation.4 | async-start | bytes 4456448 | tf_op jit(solution)/shard_map/all_gather | solution.py:55
  90.3 10.8 %all-to-all-start = ((bf16[16,1,128]{2,1,0:T(2,128)(2,1)}), bf16[16,1,128]{2,1,0:T(2,128)(2,1)S(1)}, u32[]{:S(2)}, u32[]{:S(2)}) async-start(bf16[16,1,128]{2,1,0:T(2,128)(2,1)} %stack.2), calls=%async_computation | async-start | bytes 16384 | tf_op jit(solution)/shard_map/all_to_all | solution.py:40
  93.8 297.8 %reduce-scatter.7.cloned.1.call-start = ((), (), s32[]{:S(2)}) async-start(), calls=%async_computation.8 | async-start | bytes 8912896
  174.2 3.2 copy-start
  244.8 7.3 %copy-start.1 = (f32[8,128,2048]{2,1,0:T(8,128)S(1)}, f32[8,128,2048]{2,1,0:T(8,128)}, u32[]{:S(2)}) copy-start(f32[8,128,2048]{2,1,0:T(8,128)} %copy-done) | copy-start | bytes 25165828
  257.3 2.0 copy-start.2
  283.1 109.8 %copy-start.4 = (f32[1024]{0:T(1024)S(1)}, f32[1024]{0:T(1024)}, u32[]{:S(2)}) copy-start(f32[1024]{0:T(1024)} %param.9) | copy-start | bytes 12292
  283.1 191.3 %reduce-scatter.5.cloned.1.call-start = ((), (), s32[]{:S(2)}) async-start(), calls=%async_computation.5 | async-start | bytes 6684672 | tf_op jit(solution)/shard_map/reduce_scatter | solution.py:168
  397.6 228.9 %all-reduce.2.cloned.1.call-start = ((), (), s32[]{:S(2)}) async-start(), calls=%async_computation.6 | async-start | bytes 786432 | tf_op jit(solution)/shard_map/psum | solution.py:178
Sparse Core Ops, SparseCore 0:
  9.8 70.2 all-gather.9
  89.0 73.5 all-gather.5
  165.0 73.2 all-gather.7
  283.2 108.3 reduce-scatter.6
  397.7 76.6 reduce-scatter.4
  476.9 149.4 all-reduce.1
